TPU v7x, 128 devices: a whole 4x4x4 slice. The times are simulated.
128 devices in a mesh: comp: 2 (over z_hi), mr: 64 (over z_lo, y, x, core).
Axes of the slice: x: 4, y: 4, z: 4 (z_hi: 2, z_lo: 2; z = z_hi * 2 + z_lo), core: 2. Of those that a mesh axis runs over, the one named last changes fastest.
Arguments:
- spectrum: float32 [2, 1024, 2, 64, 512], P('comp', 'mr'), may hold values from -6 to 6
- radial_basis: bfloat16 [1024, 1024, 512], P('mr'), may hold values from -0.25 to 0.25
- cutoff: int32 [1024], P('mr'), may hold values from 128 to 512, as said below
- couplings: float32 [2, 2], replicated, may hold values from 0.5 to 1.5
- trap_potential: float32 [1024], replicated, may hold values from 0 to 2
- weights: float32 [1024], replicated, may hold values from 0.25 to 0.75
Outputs:
- evolved: float32 [2, 1024, 2, 64, 512], P('comp', 'mr')
Inputs may be any that keep to these rules, and one draw needn't show every extreme that they name: cutoff[m] is the number of Laguerre degrees kept for angular mode m; degrees from cutoff[m] on are dropped.
All inputs are finite; a program needn't handle non-finite values.
Results may differ from a plain program's by a relative error of at most 0.0089.
Values may be sent and summed in bfloat16 or wider, within the bound.
A program may use at most 128 MiB of HBM per device.

v0:
```python
import math
import jax
import jax.numpy as jnp
from jax import lax
from jax.sharding import PartitionSpec as P

TIMESTEP = 0.5
ROTATION = 0.7


def spectral_tables(mode_total):
    ordinal = jnp.arange(mode_total, dtype=jnp.int32)
    product = ordinal[:, None] * ordinal[None, :] % mode_total
    angles = product.astype(jnp.float32) * (2.0 * math.pi / mode_total)
    normalizer = 1.0 / math.sqrt(mode_total)
    return (
        (jnp.cos(angles) * normalizer).astype(jnp.bfloat16),
        (jnp.sin(angles) * normalizer).astype(jnp.bfloat16),
    )


def rotate(real_part, imag_part, phase_angle):
    cosine = jnp.cos(phase_angle)
    sine_value = jnp.sin(phase_angle)
    return (
        real_part * cosine + imag_part * sine_value,
        imag_part * cosine - real_part * sine_value,
    )


def forward_modes(cosine_table, sine_table, radial, planes):
    cosine_term = jnp.einsum(
        "am,rmk->rak", cosine_table, radial, preferred_element_type=jnp.float32
    )
    sine_term = jnp.einsum("am,rmk->rak", sine_table, radial, preferred_element_type=jnp.float32)
    real_part = cosine_term[..., :planes] - sine_term[..., planes:]
    imag_part = sine_term[..., :planes] + cosine_term[..., planes:]
    return (real_part, imag_part)


def inverse_modes(cosine_table, sine_table, kicked, planes):
    cosine_back = jnp.einsum(
        "am,rak->rmk", cosine_table, kicked, preferred_element_type=jnp.float32
    )
    sine_back = jnp.einsum("am,rak->rmk", sine_table, kicked, preferred_element_type=jnp.float32)
    back_real = cosine_back[..., :planes] + sine_back[..., planes:]
    back_imag = cosine_back[..., planes:] - sine_back[..., :planes]
    return jnp.concatenate([back_real, back_imag], -1)


def on_device(spectrum, radial_basis, cutoff, couplings, trap_potential, weights):
    local_modes = spectrum.shape[1]
    planes = spectrum.shape[3]
    degrees = spectrum.shape[4]
    radius_count = radial_basis.shape[1]
    mode_width = lax.axis_size("mr")
    mode_total = local_modes * mode_width
    first_mode = lax.axis_index("mr") * local_modes
    mode_ids = first_mode + jnp.arange(local_modes, dtype=jnp.int32)
    signed = jnp.where(mode_ids < mode_total // 2, mode_ids, mode_ids - mode_total).astype(
        jnp.float32
    )
    degree_ids = jnp.arange(degrees, dtype=jnp.int32)
    energy = (
        2.0 * degree_ids.astype(jnp.float32)[None, :]
        + (jnp.abs(signed) + 1.0 - ROTATION * signed)[:, None]
    )
    kinetic_phase = TIMESTEP * energy
    kept_mask = (degree_ids[None, :] < cutoff[:, None]).astype(jnp.float32)
    spin_real, spin_imag = rotate(spectrum[0, :, 0], spectrum[0, :, 1], kinetic_phase[:, None, :])
    coeffs = jnp.concatenate(
        [spin_real * kept_mask[:, None, :], spin_imag * kept_mask[:, None, :]], axis=1
    ).astype(jnp.bfloat16)
    synthesized = jnp.einsum(
        "mkn,mrn->rmk", coeffs, radial_basis, preferred_element_type=jnp.float32
    ).astype(jnp.bfloat16)
    cosine_table, sine_table = spectral_tables(mode_total)
    comp_width = lax.axis_size("comp")
    row_count = radius_count // (mode_width * comp_width)
    first_row = (lax.axis_index("comp") * mode_width + lax.axis_index("mr")) * row_count
    trap_rows = lax.dynamic_slice_in_dim(trap_potential, first_row, row_count)
    weight_rows = lax.dynamic_slice_in_dim(weights, first_row, row_count)
    everyone = ("comp", "mr")
    radial = lax.all_to_all(synthesized, everyone, split_axis=0, concat_axis=1, tiled=True)
    radial = radial.reshape(row_count * comp_width, mode_total, 2 * planes)
    real_part, imag_part = forward_modes(cosine_table, sine_table, radial, planes)
    density = (real_part * real_part + imag_part * imag_part).reshape(
        row_count, comp_width, mode_total, planes
    )
    phase_angle = TIMESTEP * (
        couplings[:, 0][None, :, None, None] * density
        + couplings[:, 1][None, :, None, None] * density[:, ::-1]
        + trap_rows[:, None, None, None]
    )
    kick_real, kick_imag = rotate(real_part, imag_part, phase_angle.reshape(real_part.shape))
    kicked = jnp.concatenate([kick_real, kick_imag], -1).astype(jnp.bfloat16)
    back = inverse_modes(cosine_table, sine_table, kicked, planes)
    back = back.reshape(row_count, comp_width * mode_total, 2 * planes)
    analysis_input = (back * weight_rows[:, None, None]).astype(jnp.bfloat16)
    gathered_modes = lax.all_to_all(
        analysis_input, everyone, split_axis=1, concat_axis=0, tiled=True
    )
    evolved = (
        jnp.einsum("rmk,mrn->mkn", gathered_modes, radial_basis, preferred_element_type=jnp.float32)
        * kept_mask[:, None, :]
    )
    return evolved.reshape(1, local_modes, 2, planes, degrees)


def solution(mesh):
    in_specs = (P("comp", "mr", None, None, None), P("mr", None, None), P("mr"), P(), P(), P())
    out_specs = P("comp", "mr", None, None, None)
    return jax.shard_map(
        on_device, mesh=mesh, in_specs=in_specs, out_specs=out_specs, check_vma=False
    )
```

profile of v0, /device:TPU:1, one launch (start us, length us, event | category | flops | bytes accessed | tf_op | source)
XLA Modules:
  0.0 319.5 jit_solution(5036196517199933014)
XLA Ops:
  0.0 0.7 fusion.34
  0.7 0.2 fusion.33
  0.9 3.0 fusion.22
  4.0 17.4 %convert_bitcast_fusion = bf16[1024,16,128]{0,2,1:T(8,128)(2,1)} fusion(bf16[16,1024,512]{2,1,0:T(8,128)(2,1)} %param.7, bf16[16,64,512]{2,1,0:T(8,128)(2,1)S(1)} %get-tuple-element.12, bf16[16,64,512]{2,1,0:T(8,128)(2,1)S(1)} %get-tuple-element.11), kind=kOutput, calls=%fused_computation.30 | convolution fusion | flops 2153775104 | bytes 23068672 | tf_op jit(solution)/shard_map/mkn,mrn->rmk/dot_general | solution.py:74
  21.3 6.9 %copy.20 = bf16[1024,16,128]{2,1,0:T(8,128)(2,1)} copy(bf16[1024,16,128]{0,2,1:T(8,128)(2,1)} %convert_bitcast_fusion) | data formatting | bytes 8388608 | tf_op jit(solution)/shard_map/convert_element_type | solution.py:76
  28.2 0.0 copy-start.2
  28.2 12.4 %all-to-all-start = ((bf16[1024,16,128]{2,1,0:T(8,128)(2,1)}), bf16[1024,16,128]{2,1,0:T(8,128)(2,1)}, u32[]{:S(2)}, u32[]{:S(2)}) async-start(bf16[1024,16,128]{2,1,0:T(8,128)(2,1)} %copy.20), calls=%async_computation | async-start | bytes 8388608 | tf_op jit(solution)/shard_map/all_to_all | solution.py:84
  40.7 0.8 dynamic_slice.6
  41.4 0.8 dynamic_slice.7
  42.2 0.0 copy-done.2
  42.2 0.2 slice_reduce_fusion.1
  42.4 50.7 %all-to-all-done = bf16[1024,16,128]{2,1,0:T(8,128)(2,1)} async-done(((bf16[1024,16,128]{2,1,0:T(8,128)(2,1)}), bf16[1024,16,128]{2,1,0:T(8,128)(2,1)}, u32[]{:S(2)}, u32[]{:S(2)}) %all-to-all-start) | async-done | bytes 4194336 | tf_op jit(solution)/shard_map/all_to_all | solution.py:84
  93.1 2.9 copy.21
  96.1 21.4 %convolution_bitcast_fusion.2 = f32[16,1024,128]{1,2,0:T(8,128)S(1)} fusion(bf16[16,1024,128]{2,1,0:T(8,128)(2,1)S(1)} %bitcast.85), kind=kOutput, calls=%fused_computation.34 | convolution fusion | flops 4311744512 | bytes 12582912 | tf_op jit(solution)/shard_map/am,rmk->rak/dot_general | solution.py:35
  117.4 21.3 %convolution_bitcast_fusion.3 = f32[16,1024,128]{1,2,0:T(8,128)S(1)} fusion(bf16[16,1024,128]{2,1,0:T(8,128)(2,1)S(1)} %bitcast.86), kind=kOutput, calls=%fused_computation.35 | convolution fusion | flops 4311744512 | bytes 12582912 | tf_op jit(solution)/shard_map/am,rmk->rak/dot_general | solution.py:32
  138.8 2.5 multiply_add_fusion
  141.3 15.3 %fusion.14 = (f32[8,2,1024,64]{2,3,1,0:T(8,128)S(1)}, f32[8,2,1024,64]{2,3,1,0:T(8,128)S(1)}) fusion(f32[8,2,1024,64]{2,3,1,0:T(8,128)S(1)} %bitcast.83, f32[8]{0:T(128)S(1)} %dynamic_slice.6, f32[2]{0:T(128)S(1)} %get-tuple-element.6, f32[2]{0:T(128)S(1)} %get-tuple-element.5), kind=kLoop, calls=%fused_computation.37 | loop fusion | flops 5242880 | bytes 12582960 | tf_op jit(solution)/shard_map/cos | solution.py:23
  156.6 5.4 %fusion.5 = (bf16[16,1024,64]{1,2,0:T(8,128)(2,1)}, bf16[16,1024,64]{1,2,0:T(8,128)(2,1)}) fusion(f32[8,2,1024,64]{2,3,1,0:T(8,128)S(1)} %get-tuple-element.14, f32[8,2,1024,64]{2,3,1,0:T(8,128)S(1)} %get-tuple-element.13, f32[16,1024,128]{1,2,0:T(8,128)S(1)} %convolution_bitcast_fusion.2, f32[16,1024,128]{1,2,0:T(8,128)S(1)} %convolution_bitcast_fusion.3), kind=kLoop, calls=%fused_computation.17 | loop fusion | flops 10485760 | bytes 29360128 | tf_op jit(solution)/shard_map/convert
  162.0 0.0 copy-start
  162.0 0.0 copy-start.1
  162.0 23.7 %convolution_bitcast_fusion = f32[16,1024,128]{1,2,0:T(8,128)} fusion(bf16[16,1024,64]{1,2,0:T(8,128)(2,1)} %get-tuple-element.8, bf16[16,1024,64]{1,2,0:T(8,128)(2,1)} %get-tuple-element.7), kind=kOutput, calls=%fused_computation.32 | convolution fusion | flops 4320133120 | bytes 12582912 | tf_op jit(solution)/shard_map/am,rak->rmk/dot_general | solution.py:45
  185.7 0.0 copy-done
  185.7 0.0 copy-done.1
  185.7 21.5 %convolution_bitcast_fusion.1 = f32[16,1024,128]{1,2,0:T(8,128)} fusion(bf16[16,1024,64]{1,2,0:T(8,128)(2,1)S(1)} %copy-done.1, bf16[16,1024,64]{1,2,0:T(8,128)(2,1)S(1)} %copy-done), kind=kOutput, calls=%fused_computation.33 | convolution fusion | flops 4320133120 | bytes 12582912 | tf_op jit(solution)/shard_map/am,rak->rmk/dot_general | solution.py:42
  207.2 10.5 %slice_add_fusion = (f32[16,1024,64]{1,2,0:T(8,128)S(1)}, f32[16,1024,64]{1,2,0:T(8,128)}) fusion(f32[16,1024,128]{1,2,0:T(8,128)} %convolution_bitcast_fusion, f32[16,1024,128]{1,2,0:T(8,128)} %convolution_bitcast_fusion.1), kind=kLoop, calls=%fused_computation.10 | loop fusion | flops 2097152 | bytes 25165824 | tf_op jit(solution)/shard_map/add | solution.py:46
  217.7 6.8 %pad_maximum_fusion = f32[16,1024,128]{1,2,0:T(8,128)} fusion(f32[16,1024,64]{1,2,0:T(8,128)} %get-tuple-element.10, f32[16,1024,64]{1,2,0:T(8,128)S(1)} %get-tuple-element.9), kind=kLoop, calls=%fused_computation | loop fusion | flops 2097152 | bytes 16777216 | tf_op jit(solution)/shard_map/concatenate | solution.py:48
  224.5 9.2 %copy.24 = f32[16,1024,128]{2,1,0:T(8,128)} copy(f32[16,1024,128]{1,2,0:T(8,128)} %pad_maximum_fusion) | data formatting | bytes 16777216 | tf_op jit(solution)/shard_map/concatenate | solution.py:48
  233.8 4.1 %fusion = bf16[8,2048,128]{2,1,0:T(8,128)(2,1)S(1)} fusion(f32[8]{0:T(128)S(1)} %dynamic_slice.7, f32[8,2048,128]{2,1,0:T(8,128)} %bitcast.81), kind=kLoop, calls=%fused_computation.2 | loop fusion | flops 4194304 | bytes 12582944 | tf_op jit(solution)/shard_map/convert_element_type | solution.py:99
  237.9 11.9 %copy.25 = bf16[8,2048,128]{2,0,1:T(8,128)(2,1)S(1)} copy(bf16[8,2048,128]{2,1,0:T(8,128)(2,1)S(1)} %fusion) | data formatting | bytes 8388608 | tf_op jit(solution)/shard_map/convert_element_type | solution.py:99
  249.8 57.1 %all_to_all.33 = bf16[8,2048,128]{2,0,1:T(8,128)(2,1)S(1)} all-to-all(bf16[8,2048,128]{2,0,1:T(8,128)(2,1)S(1)} %copy.25), channel_id=1, replica_groups=mesh['comp'=2,'mr'=64] {'comp','mr'}, dimensions={1} | all-to-all | bytes 8388608 | tf_op jit(solution)/shard_map/all_to_all | solution.py:100
  306.9 1.4 copy.27
  308.3 11.0 %broadcast_multiply_fusion = f32[16,128,512]{2,1,0:T(8,128)} fusion(f32[16,512]{1,0:T(8,128)S(1)} %fusion.34, bf16[16,1024,512]{2,1,0:T(8,128)(2,1)} %param.7, bf16[1024,16,128]{2,1,0:T(8,128)(2,1)S(1)} %bitcast.82), kind=kOutput, calls=%fused_computation.53 | convolution fusion | flops 2148532224 | bytes 25198592 | tf_op jit(solution)/shard_map/rmk,mrn->mkn/dot_general | solution.py:104
  (2 shorter events, 0.0 us)
Async XLA Ops:
  28.2 14.0 %copy-start.2 = (f32[2,2]{1,0:T(2,128)S(1)}, f32[2,2]{1,0:T(2,128)}, u32[]{:S(2)}) copy-start(f32[2,2]{1,0:T(2,128)} %param.9) | copy-start | bytes 52
  28.2 64.9 %all-to-all-start = ((bf16[1024,16,128]{2,1,0:T(8,128)(2,1)}), bf16[1024,16,128]{2,1,0:T(8,128)(2,1)}, u32[]{:S(2)}, u32[]{:S(2)}) async-start(bf16[1024,16,128]{2,1,0:T(8,128)(2,1)} %copy.20), calls=%async_computation | async-start | bytes 8388608 | tf_op jit(solution)/shard_map/all_to_all | solution.py:84
  162.0 23.7 %copy-start = (bf16[16,1024,64]{1,2,0:T(8,128)(2,1)S(1)}, bf16[16,1024,64]{1,2,0:T(8,128)(2,1)}, u32[]{:S(2)}) copy-start(bf16[16,1024,64]{1,2,0:T(8,128)(2,1)} %get-tuple-element.7) | copy-start | bytes 6291460
  162.0 23.7 %copy-start.1 = (bf16[16,1024,64]{1,2,0:T(8,128)(2,1)S(1)}, bf16[16,1024,64]{1,2,0:T(8,128)(2,1)}, u32[]{:S(2)}) copy-start(bf16[16,1024,64]{1,2,0:T(8,128)(2,1)} %get-tuple-element.8) | copy-start | bytes 6291460
where the time goes:
time: 324 us; the launch traced here: 320 us
  matrix products  116 us (36%)
  blocking collectives  57.1 us (18%)
  waiting for transfers between devices  50.7 us (16%)
  other arithmetic  48.6 us (15%)
  local copies, waits for them, and re-layouts  34.1 us (11%)
  starting transfers between devices  12.4 us (4%)
    all_to_all x1, blocking collectives, on_device(): lax.all_to_all(analysis_input, everyone, split_axis=1, concat_axis=0, til...  57.1 us
    all_to_all x1, waiting for transfers between devices, on_device(): lax.all_to_all(synthesized, everyone, split_axis=0, concat_axis=1, tiled=...  50.7 us
    dot_general x1, matrix products, inverse_modes(): jnp.einsum('am,rak->rmk', sine_table, kicked, preferred_element_type=jnp....  23.7 us
    dot_general x1, matrix products, inverse_modes(): jnp.einsum('am,rak->rmk', cosine_table, kicked, preferred_element_type=jn...  21.5 us
    dot_general x1, matrix products, forward_modes(): jnp.einsum('am,rmk->rak', sine_table, radial, preferred_element_type=jnp....  21.4 us
    dot_general x1, matrix products, forward_modes(): jnp.einsum('am,rmk->rak', cosine_table, radial, preferred_element_type=jn...  21.3 us
    dot_general x1, matrix products, on_device(): jnp.einsum('mkn,mrn->rmk', coeffs, radial_basis, preferred_element_type=j...  17.4 us
    cos x2, other arithmetic, rotate(): cosine = jnp.cos(phase_angle)  15.5 us
  transfers between devices with their start and end apart: 1, of which 1 were waited for; matrix products, arithmetic and copies ran while one was open for 1% of the time, Pallas kernels for 0%

commit v1 on v0

--- a/solution.py
+++ b/solution.py
@@ -97,8 +97,11 @@
     back = inverse_modes(cosine_table, sine_table, kicked, planes)
     back = back.reshape(row_count, comp_width * mode_total, 2 * planes)
     analysis_input = (back * weight_rows[:, None, None]).astype(jnp.bfloat16)
-    gathered_modes = lax.all_to_all(
-        analysis_input, everyone, split_axis=1, concat_axis=0, tiled=True
+    gathered_modes = jnp.concatenate(
+        lax.all_to_all(
+            jnp.stack(jnp.split(analysis_input, lax.axis_size(everyone), axis=1)), everyone, 0, 0
+        ),
+        axis=0,
     )
     evolved = (
         jnp.einsum("rmk,mrn->mkn", gathered_modes, radial_basis, preferred_element_type=jnp.float32)

time: 324 us -> 313 us (0.966)
  local copies, waits for them, and re-layouts: 34.1 us -> 22.6 us
    convert_element_type x1 -> x0, local copies, waits for them, and re-layouts: 11.9 us -> none  [on_device(): analysis_input = (back * weight_rows[:, None, None]).astype(jnp.bfloat16)]
where the time goes in v1:
time: 313 us; the launch traced here: 308 us
  matrix products  116 us (37%)
  blocking collectives  56.8 us (18%)
  waiting for transfers between devices  50.7 us (16%)
  other arithmetic  48.7 us (16%)
  local copies, waits for them, and re-layouts  22.6 us (7%)
  starting transfers between devices  12.3 us (4%)
    all_to_all x1, blocking collectives, on_device(): lax.all_to_all(jnp.stack(jnp.split(analysis_input, lax.axis_size(everyone...  56.8 us
    all_to_all x1, waiting for transfers between devices, on_device(): lax.all_to_all(synthesized, everyone, split_axis=0, concat_axis=1, tiled=...  50.7 us
    dot_general x1, matrix products, inverse_modes(): jnp.einsum('am,rak->rmk', sine_table, kicked, preferred_element_type=jnp....  23.6 us
    dot_general x1, matrix products, forward_modes(): jnp.einsum('am,rmk->rak', sine_table, radial, preferred_element_type=jnp....  21.4 us
    dot_general x1, matrix products, forward_modes(): jnp.einsum('am,rmk->rak', cosine_table, radial, preferred_element_type=jn...  21.3 us
    dot_general x1, matrix products, inverse_modes(): jnp.einsum('am,rak->rmk', cosine_table, kicked, preferred_element_type=jn...  21.3 us
    dot_general x1, matrix products, on_device(): jnp.einsum('mkn,mrn->rmk', coeffs, radial_basis, preferred_element_type=j...  17.4 us
    cos x2, other arithmetic, rotate(): cosine = jnp.cos(phase_angle)  15.5 us
  transfers between devices with their start and end apart: 1, of which 1 were waited for; matrix products, arithmetic and copies ran while one was open for 1% of the time, Pallas kernels for 0%

profile of v1, /device:TPU:1, one launch (start us, length us, event | category | flops | bytes accessed | tf_op | source)
XLA Modules:
  0.0 308.4 jit_solution(14576754555061925891)
XLA Ops:
  0.0 0.7 fusion.34
  0.7 0.2 fusion.33
  0.9 3.0 fusion.22
  4.0 17.4 %convert_bitcast_fusion = bf16[1024,16,128]{0,2,1:T(8,128)(2,1)} fusion(bf16[16,1024,512]{2,1,0:T(8,128)(2,1)} %param.7, bf16[16,64,512]{2,1,0:T(8,128)(2,1)S(1)} %get-tuple-element.12, bf16[16,64,512]{2,1,0:T(8,128)(2,1)S(1)} %get-tuple-element.11), kind=kOutput, calls=%fused_computation.30 | convolution fusion | flops 2153775104 | bytes 23068672 | tf_op jit(solution)/shard_map/mkn,mrn->rmk/dot_general | solution.py:74
  21.3 6.9 %copy.146 = bf16[1024,16,128]{2,1,0:T(8,128)(2,1)} copy(bf16[1024,16,128]{0,2,1:T(8,128)(2,1)} %convert_bitcast_fusion) | data formatting | bytes 8388608 | tf_op jit(solution)/shard_map/convert_element_type | solution.py:76
  28.2 0.0 copy-start.2
  28.2 12.3 %all-to-all-start = ((bf16[1024,16,128]{2,1,0:T(8,128)(2,1)}), bf16[1024,16,128]{2,1,0:T(8,128)(2,1)}, u32[]{:S(2)}, u32[]{:S(2)}) async-start(bf16[1024,16,128]{2,1,0:T(8,128)(2,1)} %copy.146), calls=%async_computation | async-start | bytes 8388608 | tf_op jit(solution)/shard_map/all_to_all | solution.py:84
  40.6 0.8 dynamic_slice.6
  41.4 0.8 dynamic_slice.7
  42.1 0.0 copy-done.2
  42.1 0.2 slice_reduce_fusion.1
  42.3 50.7 %all-to-all-done = bf16[1024,16,128]{2,1,0:T(8,128)(2,1)} async-done(((bf16[1024,16,128]{2,1,0:T(8,128)(2,1)}), bf16[1024,16,128]{2,1,0:T(8,128)(2,1)}, u32[]{:S(2)}, u32[]{:S(2)}) %all-to-all-start) | async-done | bytes 4194336 | tf_op jit(solution)/shard_map/all_to_all | solution.py:84
  93.0 2.9 copy.147
  96.0 21.4 %convolution_bitcast_fusion.2 = f32[16,1024,128]{1,2,0:T(8,128)S(1)} fusion(bf16[16,1024,128]{2,1,0:T(8,128)(2,1)S(1)} %bitcast.593), kind=kOutput, calls=%fused_computation.34 | convolution fusion | flops 4311744512 | bytes 12582912 | tf_op jit(solution)/shard_map/am,rmk->rak/dot_general | solution.py:35
  117.4 21.3 %convolution_bitcast_fusion.3 = f32[16,1024,128]{1,2,0:T(8,128)S(1)} fusion(bf16[16,1024,128]{2,1,0:T(8,128)(2,1)S(1)} %bitcast.594), kind=kOutput, calls=%fused_computation.35 | convolution fusion | flops 4311744512 | bytes 12582912 | tf_op jit(solution)/shard_map/am,rmk->rak/dot_general | solution.py:32
  138.7 2.3 multiply_add_fusion
  140.9 15.3 %fusion.14 = (f32[8,2,1024,64]{2,3,1,0:T(8,128)S(1)}, f32[8,2,1024,64]{2,3,1,0:T(8,128)S(1)}) fusion(f32[8,2,1024,64]{2,3,1,0:T(8,128)S(1)} %bitcast.592, f32[8]{0:T(128)S(1)} %dynamic_slice.6, f32[2]{0:T(128)S(1)} %get-tuple-element.6, f32[2]{0:T(128)S(1)} %get-tuple-element.5), kind=kLoop, calls=%fused_computation.37 | loop fusion | flops 5242880 | bytes 12582960 | tf_op jit(solution)/shard_map/cos | solution.py:23
  156.3 5.6 %fusion.5 = (bf16[16,1024,64]{1,2,0:T(8,128)(2,1)}, bf16[16,1024,64]{1,2,0:T(8,128)(2,1)}) fusion(f32[8,2,1024,64]{2,3,1,0:T(8,128)S(1)} %get-tuple-element.14, f32[8,2,1024,64]{2,3,1,0:T(8,128)S(1)} %get-tuple-element.13, f32[16,1024,128]{1,2,0:T(8,128)S(1)} %convolution_bitcast_fusion.2, f32[16,1024,128]{1,2,0:T(8,128)S(1)} %convolution_bitcast_fusion.3), kind=kLoop, calls=%fused_computation.17 | loop fusion | flops 10485760 | bytes 29360128 | tf_op jit(solution)/shard_map/convert
  161.9 0.0 copy-start
  162.0 0.0 copy-start.1
  162.0 23.6 %convolution_bitcast_fusion = f32[16,1024,128]{1,2,0:T(8,128)} fusion(bf16[16,1024,64]{1,2,0:T(8,128)(2,1)} %get-tuple-element.8, bf16[16,1024,64]{1,2,0:T(8,128)(2,1)} %get-tuple-element.7), kind=kOutput, calls=%fused_computation.32 | convolution fusion | flops 4320133120 | bytes 12582912 | tf_op jit(solution)/shard_map/am,rak->rmk/dot_general | solution.py:45
  185.6 0.0 copy-done
  185.6 0.0 copy-done.1
  185.6 21.3 %convolution_bitcast_fusion.1 = f32[16,1024,128]{1,2,0:T(8,128)} fusion(bf16[16,1024,64]{1,2,0:T(8,128)(2,1)S(1)} %copy-done.1, bf16[16,1024,64]{1,2,0:T(8,128)(2,1)S(1)} %copy-done), kind=kOutput, calls=%fused_computation.33 | convolution fusion | flops 4320133120 | bytes 12582912 | tf_op jit(solution)/shard_map/am,rak->rmk/dot_general | solution.py:42
  206.9 10.6 %slice_add_fusion = (f32[16,1024,64]{1,2,0:T(8,128)S(1)}, f32[16,1024,64]{1,2,0:T(8,128)}) fusion(f32[16,1024,128]{1,2,0:T(8,128)} %convolution_bitcast_fusion, f32[16,1024,128]{1,2,0:T(8,128)} %convolution_bitcast_fusion.1), kind=kLoop, calls=%fused_computation.10 | loop fusion | flops 2097152 | bytes 25165824 | tf_op jit(solution)/shard_map/add | solution.py:46
  217.5 6.8 %pad_maximum_fusion = f32[16,1024,128]{1,2,0:T(8,128)} fusion(f32[16,1024,64]{1,2,0:T(8,128)} %get-tuple-element.10, f32[16,1024,64]{1,2,0:T(8,128)S(1)} %get-tuple-element.9), kind=kLoop, calls=%fused_computation | loop fusion | flops 2097152 | bytes 16777216 | tf_op jit(solution)/shard_map/concatenate | solution.py:48
  224.3 9.2 %copy.150 = f32[16,1024,128]{2,1,0:T(8,128)} copy(f32[16,1024,128]{1,2,0:T(8,128)} %pad_maximum_fusion) | data formatting | bytes 16777216 | tf_op jit(solution)/shard_map/concatenate | solution.py:48
  233.6 4.1 %fusion = bf16[8,2048,128]{2,1,0:T(8,128)(2,1)S(1)} fusion(f32[8]{0:T(128)S(1)} %dynamic_slice.7, f32[8,2048,128]{2,1,0:T(8,128)} %bitcast.590), kind=kLoop, calls=%fused_computation.2 | loop fusion | flops 4194304 | bytes 12582944 | tf_op jit(solution)/shard_map/convert_element_type | solution.py:99
  240.1 56.8 %all_to_all.20 = bf16[128,8,16,128]{3,2,1,0:T(8,128)(2,1)S(1)} all-to-all(bf16[128,8,16,128]{3,2,1,0:T(8,128)(2,1)S(1)} %constant_dynamic-update-slice_fusion), channel_id=1, replica_groups=mesh['comp'=2,'mr'=64] {'comp','mr'}, dimensions={0} | all-to-all | bytes 8388608 | tf_op jit(solution)/shard_map/all_to_all | solution.py:101
  296.9 11.0 %broadcast_multiply_fusion = f32[16,128,512]{2,1,0:T(8,128)} fusion(f32[16,512]{1,0:T(8,128)S(1)} %fusion.34, bf16[16,1024,512]{2,1,0:T(8,128)(2,1)} %param.7, bf16[1024,16,128]{2,1,0:T(8,128)(2,1)S(1)} %bitcast.591), kind=kOutput, calls=%fused_computation.53 | convolution fusion | flops 2148532224 | bytes 25198592 | tf_op jit(solution)/shard_map/rmk,mrn->mkn/dot_general | solution.py:107
  (130 shorter events, 1.8 us)
Async XLA Ops:
  28.2 13.9 %copy-start.2 = (f32[2,2]{1,0:T(2,128)S(1)}, f32[2,2]{1,0:T(2,128)}, u32[]{:S(2)}) copy-start(f32[2,2]{1,0:T(2,128)} %param.9) | copy-start | bytes 52
  28.2 64.8 %all-to-all-start = ((bf16[1024,16,128]{2,1,0:T(8,128)(2,1)}), bf16[1024,16,128]{2,1,0:T(8,128)(2,1)}, u32[]{:S(2)}, u32[]{:S(2)}) async-start(bf16[1024,16,128]{2,1,0:T(8,128)(2,1)} %copy.146), calls=%async_computation | async-start | bytes 8388608 | tf_op jit(solution)/shard_map/all_to_all | solution.py:84
  161.9 23.7 %copy-start = (bf16[16,1024,64]{1,2,0:T(8,128)(2,1)S(1)}, bf16[16,1024,64]{1,2,0:T(8,128)(2,1)}, u32[]{:S(2)}) copy-start(bf16[16,1024,64]{1,2,0:T(8,128)(2,1)} %get-tuple-element.7) | copy-start | bytes 6291460
  162.0 23.6 %copy-start.1 = (bf16[16,1024,64]{1,2,0:T(8,128)(2,1)S(1)}, bf16[16,1024,64]{1,2,0:T(8,128)(2,1)}, u32[]{:S(2)}) copy-start(bf16[16,1024,64]{1,2,0:T(8,128)(2,1)} %get-tuple-element.8) | copy-start | bytes 6291460
